TPU v7x, 256 devices: a whole 4x4x8 slice. The times are simulated.
256 devices in a mesh: prompt: 8 (over x, y_hi), tile: 32 (over y_lo, z, core).
Axes of the slice: x: 4, y: 4 (y_hi: 2, y_lo: 2; y = y_hi * 2 + y_lo), z: 8, core: 2. Of those that a mesh axis runs over, the one named last changes fastest.
Arguments:
- latent: bfloat16 [1024, 160, 16], P(('prompt', 'tile')), parts along dimension 0, may hold values from -6 to 6
- cached_latent: bfloat16 [2, 1024, 160, 16], P(None, ('prompt', 'tile')), parts along dimension 1, may hold values from -6 to 6
- cached_features: bfloat16 [2, 1024, 160, 384], P(None, ('prompt', 'tile')), parts along dimension 1, may hold values from -5 to 5
- reward_grad: bfloat16 [2048, 320, 192], P(('prompt', 'tile')), parts along dimension 0, may hold values from -6 to 6
- conv_in_weight: bfloat16 [3, 3, 3, 16, 384], replicated, may hold values from -0.3125 to 0.3125
- conv_mid_weight: bfloat16 [3, 3, 3, 384, 384], replicated, may hold values from -0.0625 to 0.0625
- conv_up_weight: bfloat16 [3, 3, 384, 192], replicated, may hold values from -0.109375 to 0.109375
- norm_gain: float32 [384], replicated, may hold values from 0.5 to 1.5
- out_gain: float32 [192], replicated, may hold values from 0.5 to 1.5
- shard_order: int32 [256], P('prompt'), parts along dimension 0, may hold values from 0 to 31, each once
Outputs:
- token_grad: float32 [40960, 64], P(('prompt', 'tile')), parts along dimension 0
There are 8 independent parts, one for each index of `prompt`. A program takes and returns all parts, laid end to end along the dimension named above; an argument that names none is the same for every part. Nothing has to cross between parts.
Inputs may be any that keep to these rules, and one draw needn't show every extreme that they name: shard_order is a permutation: each of 0 to 31 once.
All inputs are finite; a program needn't handle non-finite values.
Results may differ from a plain program's by a relative error of at most 0.0095.
Values may be sent and summed in bfloat16 or wider, within the bound.
A program may use at most 64 MiB of HBM per device.

v0:
```python
import jax
import jax.numpy as jnp
from jax import lax
from jax.experimental import pallas as pl
from jax.experimental.pallas import tpu as pltpu
from jax.sharding import PartitionSpec as P

EPS = 1e-06
F32 = jnp.float32
BF16 = jnp.bfloat16
ROWS = 4
COLS = 160
LAT = 16
MID = 384
OUT = 192
TILES = 32
PIECE = 5
TOK = 80


def iota(shape, dim):
    return lax.broadcasted_iota(jnp.int32, shape, dim)


def down(x):
    return jnp.where(iota(x.shape, 0) == 0, 0.0, pltpu.roll(x, 1, 0))


def up(x):
    n = x.shape[0]
    return jnp.where(iota(x.shape, 0) == n - 1, 0.0, pltpu.roll(x, n - 1, 0))


def mixed(x, low, high):
    a, b, c = x[:, :128], x[:, 128:256], x[:, 256:]
    middle = jnp.where(iota(b.shape, 1) < 64, low(b), high(b))
    return jnp.concatenate([low(a), middle, high(c)], axis=1)


def halves_mean(x):
    a, b, c = x[:, :128], x[:, 128:256], x[:, 256:]
    left = iota(b.shape, 1) < 64
    first = jnp.sum(a + jnp.where(left, b, 0.0), axis=1, keepdims=True) * (1.0 / OUT)
    second = jnp.sum(c + jnp.where(left, 0.0, b), axis=1, keepdims=True) * (1.0 / OUT)
    return first, second


def spread(first, second, rows):
    left = iota((rows, 128), 1) < 64
    one = jnp.broadcast_to(first, (rows, 128))
    two = jnp.broadcast_to(second, (rows, 128))
    return jnp.concatenate([one, jnp.where(left, one, two), two], axis=1)


def sigmoid(x):
    return 0.5 + 0.5 * jnp.tanh(0.5 * x)


def cotangent(normed, gain, grad):
    u = normed * gain
    s = sigmoid(u)
    return grad * gain * (s * (1.0 + u * (1.0 - s)))


def dot(a, b):
    return jnp.dot(a, b, preferred_element_type=F32)


def dot_t(a, b):
    return lax.dot_general(a, b, (((1,), (1,)), ((), ())), preferred_element_type=F32)


def kernel(
    lat_in, latc_in, feat_in, rew_in, win_in, wmid_in, wup_in, gain_ref, ogain_ref, order_ref,
    out_ref,
    lat, feat, hid, xs, rew, rewf, rewp, win, wmid, wback, wup, fold, vt,
    psend, precv, bg, zs, tsend, trecv, place,
    local_sem, halo_send, halo_recv, x_send, x_recv, p_send, p_recv, b_send, b_recv,
    t_send, t_recv, know_sem,
):
    me = lax.axis_index("tile")

    def at(offset):
        return {"tile": lax.rem(me + (offset + TILES), TILES)}

    def signal(sem, offset):
        pl.semaphore_signal(sem, inc=1, device_id=at(offset), device_id_type=pl.DeviceIdType.MESH)

    def remote(src, dst, send, recv, offset):
        return pltpu.make_async_remote_copy(
            src_ref=src, dst_ref=dst, send_sem=send, recv_sem=recv,
            device_id=at(offset), device_id_type=pl.DeviceIdType.MESH,
        )

    local = []

    def load(src, dst):
        copy = pltpu.make_async_copy(src, dst, local_sem.at[len(local)])
        copy.start()
        local.append(copy)
        return copy

    barrier = pltpu.get_barrier_semaphore()
    signal(barrier, -1)
    signal(barrier, 1)
    load_lat = [
        load(lat_in, lat.at[2, pl.ds(2, ROWS)]),
        load(latc_in, lat.at[pl.ds(0, 2), pl.ds(2, ROWS)]),
    ]
    load_win = load(win_in, win)
    load_wup = load(wup_in, wup)
    load_rew = load(rew_in, rew)
    load_feat = load(feat_in, feat.at[pl.ds(0, 2), pl.ds(1, ROWS)])
    load_mid = []
    for t in (0, 1, 2):
        for j in range(3):
            load_mid.append(load(wmid_in.at[t, :, j], wmid.at[t, :, :, pl.ds(j * MID, MID)]))
    load_back = []
    for i in range(3):
        load_back.append(load(wmid_in.at[2, i], wback.at[:, :, pl.ds(i * MID, MID)]))

    pl.semaphore_wait(barrier, 2)
    halo = []
    for side, offset in ((0, -1), (1, 1)):
        row = 0 if side == 0 else ROWS - 2
        land = ROWS + 2 if side == 0 else 0
        copies = [
            remote(lat_in.at[pl.ds(row, 2)], lat.at[2, pl.ds(land, 2)],
                   halo_send.at[side, 0], halo_recv.at[side, 0], offset),
            remote(latc_in.at[:, pl.ds(row, 2)], lat.at[pl.ds(0, 2), pl.ds(land, 2)],
                   halo_send.at[side, 1], halo_recv.at[side, 1], offset),
        ]
        row = 0 if side == 0 else ROWS - 1
        land = ROWS + 1 if side == 0 else 0
        copies.append(
            remote(feat_in.at[:, pl.ds(row, 1)], feat.at[pl.ds(0, 2), pl.ds(land, 1)],
                   halo_send.at[side, 2], halo_recv.at[side, 2], offset))
        halo.append(copies)
    for n in range(3):
        for side in range(2):
            halo[side][n].start()
    signal(know_sem.at[0], -1)
    signal(know_sem.at[0], 1)

    load_wup.wait()
    parts = []
    for i in range(3):
        k0, k1, k2 = (wup[i, j].astype(F32) for j in range(3))
        parts.append(jnp.concatenate(
            [jnp.concatenate([k0, k2], axis=1), jnp.concatenate([k1 + k2, k0 + k1], axis=1)],
            axis=1))
    fold[0, :MID] = parts[0].astype(BF16)
    fold[0, MID:] = (parts[1] + parts[2]).astype(BF16)
    fold[1, :MID] = (parts[0] + parts[1]).astype(BF16)
    fold[1, MID:] = parts[2].astype(BF16)

    load_rew.wait()
    rewf[1] = jnp.zeros((2 * COLS, 128), F32)
    for y in range(2 * ROWS):
        rewf[0] = rew[y, :, :128].astype(F32)
        rewf[1, :, :OUT - 128] = rew[y, :, 128:].astype(F32)
        e0, e1 = (rewf[n, pl.ds(0, COLS, stride=2), :] for n in range(2))
        o0, o1 = (pltpu.roll(rewf[n, pl.ds(1, COLS, stride=2), :], 64, 1) for n in range(2))
        left = iota((COLS, 128), 1) < 64
        rewp[y] = jnp.concatenate(
            [e0, jnp.where(left, e1, o0), jnp.where(left, o0, o1)], axis=1).astype(BF16)

    load_win.wait()
    r = iota((1024, 144), 0)
    par = lax.shift_right_logical(r, 9)
    d = lax.shift_right_logical(r, 7) & 3
    d = jnp.where(d == 3, -1, d)
    extra = lax.shift_right_logical(r, 6) & 1
    a = lax.shift_right_logical(r, 5) & 1
    b = lax.shift_right_logical(r, 4) & 1
    c = r & 15
    i = jnp.where(extra == 0, jnp.where(par == 0, a + 1, a), jnp.where(par == 0, 0, 2))
    fits = jnp.where(extra == 0, 1, jnp.where(par == 0, a, 1 - a))
    j = b - d + 1
    fits = jnp.where((j >= 0) & (j <= 2), fits, 0)
    want = jnp.where(fits == 1, i * 48 + j * 16 + c, -1)
    pick = jnp.where(iota((1024, 144), 1) == want, 1.0, 0.0).astype(BF16)
    vt[...] = dot(pick, win[2].reshape(144, MID)).astype(BF16)
    zs[:, :, 0:8] = jnp.zeros((ROWS, 4, 8, 128), F32)
    zs[:, :, COLS + 8:] = jnp.zeros((ROWS, 4, 8, 128), F32)

    lane = lax.shift_right_logical(iota((1, 256), 1), 3)
    own_at = jnp.full((1, 256), -1, jnp.int32)
    edge_at = jnp.full((1, 256), -1, jnp.int32)
    for t in range(TILES):
        own_at = jnp.where(lane == t, order_ref[t], own_at)
        after = order_ref[t + 1] if t + 1 < TILES else jnp.int32(-1)
        before = order_ref[t - 1] if t > 0 else jnp.int32(-1)
        edge_at = jnp.where(lane == t, jnp.where(me < TILES // 2, after, before), edge_at)
    row = iota((TILES * PIECE, 256), 0)
    block = lax.shift_right_logical(row * 205, 10)
    same = (row - block * PIECE) == (iota((TILES * PIECE, 256), 1) & 7)
    place[0] = jnp.where(same & (block == own_at), 1.0, 0.0).astype(BF16)
    place[1] = jnp.where(same & (block == edge_at), 1.0, 0.0).astype(BF16)

    for copy in load_lat:
        copy.wait()
    for n in range(2):
        for side in range(2):
            halo[side][n].wait_recv()

    @pl.when(me == 0)
    def _():
        lat[:, 0:2] = jnp.zeros((3, 2, COLS, LAT), BF16)

    @pl.when(me == TILES - 1)
    def _():
        lat[:, ROWS + 2:] = jnp.zeros((3, 2, COLS, LAT), BF16)

    taps = []
    for h in range(ROWS + 4):
        x = jnp.concatenate([lat[t, h].astype(F32) for t in range(3)], axis=1)
        taps.append(jnp.concatenate([down(x), x, up(x)], axis=1).astype(BF16))
    total = None
    for i in range(3):
        weight = jnp.concatenate([win[t, i, j] for j in range(3) for t in range(3)], axis=0)
        part = dot(jnp.concatenate(taps[i:i + ROWS + 2], axis=0), weight)
        total = part if total is None else total + part
    gain = gain_ref[...]
    for h in range(ROWS + 2):
        value = total[h * COLS:(h + 1) * COLS].astype(BF16)
        hid[h] = value
        v = value.astype(F32)
        u = v * lax.rsqrt(jnp.mean(v * v, axis=1, keepdims=True) + EPS) * gain
        feat[2, h] = (u * sigmoid(u)).astype(BF16)

    load_feat.wait()
    for side in range(2):
        halo[side][2].wait_recv()

    @pl.when(me == 0)
    def _():
        feat[:, 0] = jnp.zeros((3, COLS, MID), BF16)

    @pl.when(me == TILES - 1)
    def _():
        feat[:, ROWS + 1] = jnp.zeros((3, COLS, MID), BF16)

    for copy in load_mid:
        copy.wait()
    pl.semaphore_wait(know_sem.at[0], 2)
    signal(know_sem.at[1], -2)
    signal(know_sem.at[1], 2)

    def middle(rows):
        left = jnp.concatenate(
            [jnp.concatenate([feat[t, h + i] for t in range(3) for i in range(3)], axis=1)
             for h in rows], axis=0)
        y = dot(left, wmid[...].reshape(9 * MID, 3 * MID))
        for n, h in enumerate(rows):
            z = y[n * COLS:(n + 1) * COLS]
            value = z[:, MID:2 * MID] + down(z[:, :MID]) + up(z[:, 2 * MID:])
            xs[h + 1] = (hid[h + 1].astype(F32) + value).astype(BF16)

    middle((0, 3))
    x_up = remote(xs.at[1], xs.at[ROWS + 1], x_send.at[0], x_recv.at[0], -1)
    x_down = remote(xs.at[ROWS], xs.at[0], x_send.at[1], x_recv.at[1], 1)
    x_up.start()
    x_down.start()
    pl.semaphore_wait(know_sem.at[1], 2)
    signal(know_sem.at[2], -4)
    signal(know_sem.at[2], 4)
    middle((1, 2))
    pl.semaphore_wait(know_sem.at[2], 2)
    signal(know_sem.at[3], -8)
    signal(know_sem.at[3], 8)
    x_up.wait_recv()
    x_down.wait_recv()

    @pl.when(me == 0)
    def _():
        xs[0] = jnp.zeros((COLS, MID), BF16)

    @pl.when(me == TILES - 1)
    def _():
        xs[ROWS + 1] = jnp.zeros((COLS, MID), BF16)

    ogain = ogain_ref[...]

    def upper(a, rows):
        left = jnp.concatenate(
            [jnp.concatenate([xs[h + a], xs[h + a + 1]], axis=1) for h in rows], axis=0)
        y = dot(left, fold[a])
        lefts = []
        for n, h in enumerate(rows):
            z = y[n * COLS:(n + 1) * COLS]
            v = (z[:, MID:] + mixed(z[:, :MID], down, up)).astype(BF16).astype(F32)
            one, two = halves_mean(v * v)
            scale = spread(lax.rsqrt(one + EPS), lax.rsqrt(two + EPS), COLS)
            normed = v * scale
            t = cotangent(normed, ogain, rewp[2 * h + a].astype(F32))
            one, two = halves_mean(t * normed)
            g = (scale * (t - normed * spread(one, two, COLS))).astype(BF16)
            lefts.append(jnp.concatenate([mixed(g.astype(F32), up, down).astype(BF16), g], axis=1))
        z = dot_t(jnp.concatenate(lefts, axis=0), fold[a])
        return {h: (z[n * COLS:(n + 1) * COLS, :MID], z[n * COLS:(n + 1) * COLS, MID:])
                for n, h in enumerate(rows)}

    z0 = upper(0, (0, 1))
    psend[0] = z0[0][0].astype(BF16)
    p_up = remote(psend.at[0], precv.at[1], p_send.at[0], p_recv.at[0], -1)
    p_up.start()
    z1 = upper(1, (2, 3))
    psend[1] = z1[3][1].astype(BF16)
    p_down = remote(psend.at[1], precv.at[0], p_send.at[1], p_recv.at[1], 1)
    p_down.start()
    z0.update(upper(0, (2, 3)))
    z1.update(upper(1, (0, 1)))
    p_up.wait_recv()
    p_down.wait_recv()

    @pl.when(me == 0)
    def _():
        precv[0] = jnp.zeros((COLS, MID), BF16)

    @pl.when(me == TILES - 1)
    def _():
        precv[1] = jnp.zeros((COLS, MID), BF16)

    bg[1] = (z0[0][1] + z0[1][0] + z1[0][0] + precv[0].astype(F32)).astype(BF16)
    bg[ROWS] = (z0[3][1] + precv[1].astype(F32) + z1[3][0] + z1[2][1]).astype(BF16)
    b_up = remote(bg.at[1], bg.at[ROWS + 1], b_send.at[0], b_recv.at[0], -1)
    b_down = remote(bg.at[ROWS], bg.at[0], b_send.at[1], b_recv.at[1], 1)
    b_up.start()
    b_down.start()
    for h in (1, 2):
        bg[h + 1] = (z0[h][1] + z0[h + 1][0] + z1[h][0] + z1[h - 1][1]).astype(BF16)

    for copy in load_back:
        copy.wait()

    def lower(rows):
        left = jnp.concatenate(
            [jnp.concatenate([bg[h + 2], bg[h + 1], bg[h]], axis=1) for h in rows], axis=0)
        y = dot_t(left, wback[...].reshape(3 * MID, 3 * MID))
        for n, h in enumerate(rows):
            z = y[n * COLS:(n + 1) * COLS]
            grad = z[:, MID:2 * MID] + up(z[:, :MID]) + down(z[:, 2 * MID:])
            v = hid[h + 1].astype(F32)
            scale = lax.rsqrt(jnp.mean(v * v, axis=1, keepdims=True) + EPS)
            normed = v * scale
            t = cotangent(normed, gain, grad)
            m = jnp.mean(t * normed, axis=1, keepdims=True)
            g = (bg[h + 1].astype(F32) + scale * (t - normed * m)).astype(BF16)
            last = dot_t(g, vt[(h % 2) * 512:(h % 2) * 512 + 512])
            for p in range(4):
                zs[h, p, 8:COLS + 8] = last[:, p * 128:(p + 1) * 128]

    lower((1, 2))
    b_up.wait_recv()
    b_down.wait_recv()

    @pl.when(me == 0)
    def _():
        bg[0] = jnp.zeros((COLS, MID), BF16)

    @pl.when(me == TILES - 1)
    def _():
        bg[ROWS + 1] = jnp.zeros((COLS, MID), BF16)

    lower((0, 3))

    def tokens(h):
        picks = ((0, 0), (1, 1), (2, 2), (3, -1))
        parts = [zs[h, n, pl.ds(8 + d, TOK, stride=2), :] for n, d in picks]
        return (parts[0] + parts[1]) + (parts[2] + parts[3])

    u0, u1, u2, u3 = (tokens(h) for h in range(ROWS))
    low = iota((TOK, 128), 1) < 64
    m0 = jnp.where(low, u0 + u1 + pltpu.roll(u2, 64, 1), u3)
    m1 = jnp.where(low, u2 + u3 + pltpu.roll(u1, 64, 1), u0)
    both = jnp.concatenate([m0, m1], axis=0).astype(BF16)
    row = iota((256, TILES * PIECE), 0)
    source = lax.shift_right_logical(row, 3) * PIECE + (row & 7)
    take = ((row & 7) < PIECE) & (iota((256, TILES * PIECE), 1) == source)
    blocks = dot(jnp.where(take, 1.0, 0.0).astype(BF16), both)
    tsend[...] = blocks.reshape(TILES, 8, 128).astype(BF16)

    pl.semaphore_wait(know_sem.at[3], 2)

    def block_copy(k):
        to = lax.rem(me + k, TILES)
        return pltpu.make_async_remote_copy(
            src_ref=tsend.at[to], dst_ref=trecv.at[me], send_sem=t_send.at[k],
            recv_sem=t_recv.at[k],
            device_id={"tile": to}, device_id_type=pl.DeviceIdType.MESH)

    for k in range(1, TILES):
        block_copy(k).start()
    trecv[me] = tsend[me]
    for k in range(1, TILES):
        source = lax.rem(me + (TILES - k), TILES)
        pltpu.make_async_remote_copy(
            src_ref=tsend.at[source], dst_ref=trecv.at[source], send_sem=t_send.at[k],
            recv_sem=t_recv.at[k],
            device_id={"tile": source}, device_id_type=pl.DeviceIdType.MESH).wait_recv()
    got = trecv[...].astype(F32).reshape(TILES * 8, 128).astype(BF16)
    own = dot(place[0], got)
    edge = dot(place[1], got)
    out_ref[...] = (own + pltpu.roll(edge, 64, 1))[:, :64]

    for copies in halo:
        for copy in copies:
            copy.wait_send()
    for copy in (x_up, x_down, p_up, p_down, b_up, b_down):
        copy.wait_send()
    for k in range(1, TILES):
        block_copy(k).wait_send()


def shards(latent, cached_latent, cached_features, reward_grad, conv_in_weight, conv_mid_weight,
           conv_up_weight, norm_gain, out_gain, shard_order):
    hbm = pl.BlockSpec(memory_space=pltpu.HBM)
    vmem = pl.BlockSpec(memory_space=pltpu.VMEM)
    smem = pl.BlockSpec(memory_space=pltpu.SMEM)
    dma = pltpu.SemaphoreType.DMA
    call = pl.pallas_call(
        kernel,
        out_shape=jax.ShapeDtypeStruct((TILES * PIECE, 4 * LAT), F32),
        in_specs=[hbm] * 7 + [vmem, vmem, smem],
        out_specs=vmem,
        scratch_shapes=[
            pltpu.VMEM((3, ROWS + 4, COLS, LAT), BF16),
            pltpu.VMEM((3, ROWS + 2, COLS, MID), BF16),
            pltpu.VMEM((ROWS + 2, COLS, MID), BF16),
            pltpu.VMEM((ROWS + 2, COLS, MID), BF16),
            pltpu.VMEM((2 * ROWS, 2 * COLS, OUT), BF16),
            pltpu.VMEM((2, 2 * COLS, 128), F32),
            pltpu.VMEM((2 * ROWS, COLS, 2 * OUT), BF16),
            pltpu.VMEM((3, 3, 3, LAT, MID), BF16),
            pltpu.VMEM((3, 3, MID, 3 * MID), BF16),
            pltpu.VMEM((3, MID, 3 * MID), BF16),
            pltpu.VMEM((3, 3, MID, OUT), BF16),
            pltpu.VMEM((2, 2 * MID, 4 * OUT), BF16),
            pltpu.VMEM((1024, MID), BF16),
            pltpu.VMEM((2, COLS, MID), BF16),
            pltpu.VMEM((2, COLS, MID), BF16),
            pltpu.VMEM((ROWS + 2, COLS, MID), BF16),
            pltpu.VMEM((ROWS, 4, COLS + 16, 128), F32),
            pltpu.VMEM((TILES, 8, 128), BF16),
            pltpu.VMEM((TILES, 8, 128), BF16),
            pltpu.VMEM((2, TILES * PIECE, 256), BF16),
            dma((18,)), dma((2, 3)), dma((2, 3)), dma((2,)), dma((2,)), dma((2,)), dma((2,)),
            dma((2,)), dma((2,)), dma((TILES,)), dma((TILES,)),
            pltpu.SemaphoreType.REGULAR((4,)),
        ],
        compiler_params=pltpu.CompilerParams(
            collective_id=0, has_side_effects=True, vmem_limit_bytes=60 << 20),
    )
    return call(latent, cached_latent, cached_features, reward_grad, conv_in_weight,
                conv_mid_weight, conv_up_weight, norm_gain[None, :],
                jnp.concatenate([out_gain, out_gain])[None, :], shard_order)


def solution(mesh):
    part = P(("prompt", "tile"), None, None)
    frames = P(None, ("prompt", "tile"), None, None)
    return jax.shard_map(
        shards,
        mesh=mesh,
        in_specs=(part, frames, frames, part, P(), P(), P(), P(), P(), P("prompt")),
        out_specs=P(("prompt", "tile"), None),
        check_vma=False,
    )
```

profile of v0, /device:TPU:1, one launch (start us, length us, event | category | flops | bytes accessed | tf_op | source)
XLA Modules:
  0.0 56.6 jit_solution(7498677077414870411)
XLA Ops:
  0.0 1.2 %broadcast_in_dim.6.gain_ref = f32[1,384]{1,0:T(1,128)} reshape(f32[384]{0:T(512)} %param.17) | data formatting | bytes 3072 | tf_op jit(solution)/shard_map/broadcast_in_dim | solution.py:456
  1.2 0.8 %pad_maximum_fusion = f32[384]{0:T(512)S(1)} fusion(f32[192]{0:T(256)} %param.18), kind=kLoop, calls=%fused_computation | loop fusion | flops 384 | bytes 2304 | tf_op jit(solution)/shard_map/concatenate | solution.py:457
  2.1 0.6 %broadcast_in_dim.7.ogain_ref = f32[1,384]{1,0:T(1,128)} reshape(f32[384]{0:T(512)S(1)} %pad_maximum_fusion) | data formatting | bytes 3072 | tf_op jit(solution)/shard_map/broadcast_in_dim | solution.py:457
  2.7 1.6 %copy.11.lat_in = bf16[4,160,16]{2,1,0:T(8,128)(2,1)} copy(bf16[4,160,16]{1,2,0:T(8,128)(2,1)} %param.10) | data formatting | bytes 40960 | tf_op args[0]
  4.2 1.8 %copy.12.latc_in = bf16[2,4,160,16]{3,2,1,0:T(8,128)(2,1)} copy(bf16[2,4,160,16]{2,3,1,0:T(8,128)(2,1)} %param.11) | data formatting | bytes 81920 | tf_op args[1]
  6.0 0.0 copy-start
  6.0 2.6 %copy.13.rew_in = bf16[8,320,192]{2,1,0:T(8,128)(2,1)} copy(bf16[8,320,192]{1,2,0:T(8,128)(2,1)} %param.13) | data formatting | bytes 1966080 | tf_op args[3]
  8.6 0.0 copy-done
  8.6 2.2 %copy.14.wup_in = bf16[3,3,384,192]{3,2,1,0:T(8,128)(2,1)} copy(bf16[3,3,384,192]{2,3,1,0:T(8,128)(2,1)S(1)} %copy-done) | data formatting | bytes 2654208 | tf_op args[6]
  10.8 44.2 %shard_map.100 = f32[160,64]{1,0:T(8,128)} custom-call(bf16[4,160,16]{2,1,0:T(8,128)(2,1)} %copy.11.lat_in, bf16[2,4,160,16]{3,2,1,0:T(8,128)(2,1)} %copy.12.latc_in, bf16[2,4,160,384]{3,2,1,0:T(8,128)(2,1)} %feat_in.1, bf16[8,320,192]{2,1,0:T(8,128)(2,1)} %copy.13.rew_in, bf16[3,3,3,16,384]{4,3,2,1,0:T(8,128)(2,1)} %win_in.1, ...), custom_call_target="tpu_custom_call" | custom-call | tf_op jit(solution)/shard_map/pallas_call | solution.py:455
  55.0 1.6 %copy.15 = f32[160,64]{0,1:T(8,128)} copy(f32[160,64]{1,0:T(8,128)} %shard_map.100) | data formatting | bytes 81920 | tf_op jit(solution)/shard_map/pallas_call | solution.py:455
Async XLA Ops:
  6.0 2.6 %copy-start = (bf16[3,3,384,192]{2,3,1,0:T(8,128)(2,1)S(1)}, bf16[3,3,384,192]{2,3,1,0:T(8,128)(2,1)}, u32[]{:S(2)}) copy-start(bf16[3,3,384,192]{2,3,1,0:T(8,128)(2,1)} %param.16) | copy-start | bytes 3981316
where the time goes:
time: 56.9 us; the launch traced here: 56.6 us
  Pallas kernels  44.2 us (78%)
  local copies, waits for them, and re-layouts  11.6 us (20%)
  other arithmetic  0.83 us (1%)
    pallas_call x1, Pallas kernels, shards(): call(latent, cached_latent, cached_features, reward_grad, conv_in_weight,...  44.2 us
    unnamed x6, local copies, waits for them, and re-layouts  8.15 us
    pallas_call x1, local copies, waits for them, and re-layouts, shards(): call(latent, cached_latent, cached_features, reward_grad, conv_in_weight,...  1.6 us
    broadcast_in_dim x1, local copies, waits for them, and re-layouts, shards(): norm_gain[None, :]  1.24 us

commit v1 on v0

--- a/solution.py
+++ b/solution.py
@@ -73,7 +73,7 @@
 def kernel(
     lat_in, latc_in, feat_in, rew_in, win_in, wmid_in, wup_in, gain_ref, ogain_ref, order_ref,
     out_ref,
-    lat, feat, hid, xs, rew, rewf, rewp, win, wmid, wback, wup, fold, vt,
+    lat, feat, hid, xs, rew, rewp, win, wmid, wback, wup, fold, vt,
     psend, precv, bg, zs, tsend, trecv, place,
     local_sem, halo_send, halo_recv, x_send, x_recv, p_send, p_recv, b_send, b_recv,
     t_send, t_recv, know_sem,
@@ -146,24 +146,25 @@
     parts = []
     for i in range(3):
         k0, k1, k2 = (wup[i, j].astype(F32) for j in range(3))
-        parts.append(jnp.concatenate(
-            [jnp.concatenate([k0, k2], axis=1), jnp.concatenate([k1 + k2, k0 + k1], axis=1)],
-            axis=1))
-    fold[0, :MID] = parts[0].astype(BF16)
-    fold[0, MID:] = (parts[1] + parts[2]).astype(BF16)
-    fold[1, :MID] = (parts[0] + parts[1]).astype(BF16)
-    fold[1, MID:] = parts[2].astype(BF16)
+        parts.append(jnp.concatenate([k0, k2, k1 + k2, k0 + k1], axis=0))
+    fold[0, :, :MID] = parts[0].astype(BF16)
+    fold[0, :, MID:] = (parts[1] + parts[2]).astype(BF16)
+    fold[1, :, :MID] = (parts[0] + parts[1]).astype(BF16)
+    fold[1, :, MID:] = parts[2].astype(BF16)
 
     load_rew.wait()
-    rewf[1] = jnp.zeros((2 * COLS, 128), F32)
+    n = iota((2 * COLS, 2 * COLS), 0)
+    column = jnp.where(n < COLS, 2 * n, 2 * n - (2 * COLS - 1))
+    parting = jnp.where(iota((2 * COLS, 2 * COLS), 1) == column, 1.0, 0.0).astype(BF16)
+    left = iota((COLS, 128), 1) < 64
     for y in range(2 * ROWS):
-        rewf[0] = rew[y, :, :128].astype(F32)
-        rewf[1, :, :OUT - 128] = rew[y, :, 128:].astype(F32)
-        e0, e1 = (rewf[n, pl.ds(0, COLS, stride=2), :] for n in range(2))
-        o0, o1 = (pltpu.roll(rewf[n, pl.ds(1, COLS, stride=2), :], 64, 1) for n in range(2))
-        left = iota((COLS, 128), 1) < 64
+        flat = jnp.concatenate([rew[y], jnp.zeros((256 - OUT, 2 * COLS), BF16)], axis=0)
+        parted = dot_t(parting, flat)
+        even, odd = parted[:COLS], parted[COLS:]
+        o0, o1 = pltpu.roll(odd[:, :128], 64, 1), pltpu.roll(odd[:, 128:], 64, 1)
         rewp[y] = jnp.concatenate(
-            [e0, jnp.where(left, e1, o0), jnp.where(left, o0, o1)], axis=1).astype(BF16)
+            [even[:, :128], jnp.where(left, even[:, 128:], o0), jnp.where(left, o0, o1)],
+            axis=1).astype(BF16)
 
     load_win.wait()
     r = iota((1024, 144), 0)
@@ -184,17 +185,17 @@
     zs[:, :, 0:8] = jnp.zeros((ROWS, 4, 8, 128), F32)
     zs[:, :, COLS + 8:] = jnp.zeros((ROWS, 4, 8, 128), F32)
 
-    lane = lax.shift_right_logical(iota((1, 256), 1), 3)
-    own_at = jnp.full((1, 256), -1, jnp.int32)
-    edge_at = jnp.full((1, 256), -1, jnp.int32)
+    slot = lax.shift_right_logical(iota((256, 1), 0), 3)
+    own_at = jnp.full((256, 1), -1, jnp.int32)
+    edge_at = jnp.full((256, 1), -1, jnp.int32)
     for t in range(TILES):
-        own_at = jnp.where(lane == t, order_ref[t], own_at)
+        own_at = jnp.where(slot == t, order_ref[t], own_at)
         after = order_ref[t + 1] if t + 1 < TILES else jnp.int32(-1)
         before = order_ref[t - 1] if t > 0 else jnp.int32(-1)
-        edge_at = jnp.where(lane == t, jnp.where(me < TILES // 2, after, before), edge_at)
-    row = iota((TILES * PIECE, 256), 0)
-    block = lax.shift_right_logical(row * 205, 10)
-    same = (row - block * PIECE) == (iota((TILES * PIECE, 256), 1) & 7)
+        edge_at = jnp.where(slot == t, jnp.where(me < TILES // 2, after, before), edge_at)
+    spot = iota((256, TILES * PIECE), 1)
+    block = lax.shift_right_logical(spot * 205, 10)
+    same = (spot - block * PIECE) == (iota((256, TILES * PIECE), 0) & 7)
     place[0] = jnp.where(same & (block == own_at), 1.0, 0.0).astype(BF16)
     place[1] = jnp.where(same & (block == edge_at), 1.0, 0.0).astype(BF16)
 
@@ -206,22 +207,22 @@
 
     @pl.when(me == 0)
     def _():
-        lat[:, 0:2] = jnp.zeros((3, 2, COLS, LAT), BF16)
+        lat[:, 0:2] = jnp.zeros((3, 2, LAT, COLS), BF16)
 
     @pl.when(me == TILES - 1)
     def _():
-        lat[:, ROWS + 2:] = jnp.zeros((3, 2, COLS, LAT), BF16)
+        lat[:, ROWS + 2:] = jnp.zeros((3, 2, LAT, COLS), BF16)
 
     taps = []
     for h in range(ROWS + 4):
-        x = jnp.concatenate([lat[t, h].astype(F32) for t in range(3)], axis=1)
+        x = jnp.concatenate([lat[t, h].astype(F32) for t in range(3)], axis=0).T
         taps.append(jnp.concatenate([down(x), x, up(x)], axis=1).astype(BF16))
     total = None
     for i in range(3):
         weight = jnp.concatenate([win[t, i, j] for j in range(3) for t in range(3)], axis=0)
         part = dot(jnp.concatenate(taps[i:i + ROWS + 2], axis=0), weight)
         total = part if total is None else total + part
-    gain = gain_ref[...]
+    gain = gain_ref[...].reshape(1, MID)
     for h in range(ROWS + 2):
         value = total[h * COLS:(h + 1) * COLS].astype(BF16)
         hid[h] = value
@@ -280,12 +281,13 @@
     def _():
         xs[ROWS + 1] = jnp.zeros((COLS, MID), BF16)
 
-    ogain = ogain_ref[...]
+    ogain = ogain_ref[...].reshape(1, OUT)
+    ogain = jnp.concatenate([ogain, ogain], axis=1)
 
     def upper(a, rows):
         left = jnp.concatenate(
             [jnp.concatenate([xs[h + a], xs[h + a + 1]], axis=1) for h in rows], axis=0)
-        y = dot(left, fold[a])
+        y = dot_t(left, fold[a])
         lefts = []
         for n, h in enumerate(rows):
             z = y[n * COLS:(n + 1) * COLS]
@@ -297,7 +299,7 @@
             one, two = halves_mean(t * normed)
             g = (scale * (t - normed * spread(one, two, COLS))).astype(BF16)
             lefts.append(jnp.concatenate([mixed(g.astype(F32), up, down).astype(BF16), g], axis=1))
-        z = dot_t(jnp.concatenate(lefts, axis=0), fold[a])
+        z = dot(jnp.concatenate(lefts, axis=0), fold[a])
         return {h: (z[n * COLS:(n + 1) * COLS, :MID], z[n * COLS:(n + 1) * COLS, MID:])
                 for n, h in enumerate(rows)}
 
@@ -399,10 +401,8 @@
             src_ref=tsend.at[source], dst_ref=trecv.at[source], send_sem=t_send.at[k],
             recv_sem=t_recv.at[k],
             device_id={"tile": source}, device_id_type=pl.DeviceIdType.MESH).wait_recv()
-    got = trecv[...].astype(F32).reshape(TILES * 8, 128).astype(BF16)
-    own = dot(place[0], got)
-    edge = dot(place[1], got)
-    out_ref[...] = (own + pltpu.roll(edge, 64, 1))[:, :64]
+    got = trecv[...].astype(F32).reshape(TILES * 8, 128).T.astype(BF16)
+    out_ref[...] = dot(got[:64], place[0]) + dot(got[64:], place[1])
 
     for copies in halo:
         for copy in copies:
@@ -421,22 +421,21 @@
     dma = pltpu.SemaphoreType.DMA
     call = pl.pallas_call(
         kernel,
-        out_shape=jax.ShapeDtypeStruct((TILES * PIECE, 4 * LAT), F32),
+        out_shape=jax.ShapeDtypeStruct((4 * LAT, TILES * PIECE), F32),
         in_specs=[hbm] * 7 + [vmem, vmem, smem],
         out_specs=vmem,
         scratch_shapes=[
-            pltpu.VMEM((3, ROWS + 4, COLS, LAT), BF16),
+            pltpu.VMEM((3, ROWS + 4, LAT, COLS), BF16),
             pltpu.VMEM((3, ROWS + 2, COLS, MID), BF16),
             pltpu.VMEM((ROWS + 2, COLS, MID), BF16),
             pltpu.VMEM((ROWS + 2, COLS, MID), BF16),
-            pltpu.VMEM((2 * ROWS, 2 * COLS, OUT), BF16),
-            pltpu.VMEM((2, 2 * COLS, 128), F32),
+            pltpu.VMEM((2 * ROWS, OUT, 2 * COLS), BF16),
             pltpu.VMEM((2 * ROWS, COLS, 2 * OUT), BF16),
             pltpu.VMEM((3, 3, 3, LAT, MID), BF16),
             pltpu.VMEM((3, 3, MID, 3 * MID), BF16),
             pltpu.VMEM((3, MID, 3 * MID), BF16),
-            pltpu.VMEM((3, 3, MID, OUT), BF16),
-            pltpu.VMEM((2, 2 * MID, 4 * OUT), BF16),
+            pltpu.VMEM((3, 3, OUT, MID), BF16),
+            pltpu.VMEM((2, 4 * OUT, 2 * MID), BF16),
             pltpu.VMEM((1024, MID), BF16),
             pltpu.VMEM((2, COLS, MID), BF16),
             pltpu.VMEM((2, COLS, MID), BF16),
@@ -444,7 +443,7 @@
             pltpu.VMEM((ROWS, 4, COLS + 16, 128), F32),
             pltpu.VMEM((TILES, 8, 128), BF16),
             pltpu.VMEM((TILES, 8, 128), BF16),
-            pltpu.VMEM((2, TILES * PIECE, 256), BF16),
+            pltpu.VMEM((2, 256, TILES * PIECE), BF16),
             dma((18,)), dma((2, 3)), dma((2, 3)), dma((2,)), dma((2,)), dma((2,)), dma((2,)),
             dma((2,)), dma((2,)), dma((TILES,)), dma((TILES,)),
             pltpu.SemaphoreType.REGULAR((4,)),
@@ -452,9 +451,10 @@
         compiler_params=pltpu.CompilerParams(
             collective_id=0, has_side_effects=True, vmem_limit_bytes=60 << 20),
     )
-    return call(latent, cached_latent, cached_features, reward_grad, conv_in_weight,
-                conv_mid_weight, conv_up_weight, norm_gain[None, :],
-                jnp.concatenate([out_gain, out_gain])[None, :], shard_order)
+    out = call(jnp.swapaxes(latent, 1, 2), jnp.swapaxes(cached_latent, 2, 3), cached_features,
+               jnp.swapaxes(reward_grad, 1, 2), conv_in_weight, conv_mid_weight,
+               jnp.swapaxes(conv_up_weight, 2, 3), norm_gain, out_gain, shard_order)
+    return out.T
 
 
 def solution(mesh):

time: 56.9 us -> 43.7 us (0.77)
  local copies, waits for them, and re-layouts: 11.6 us -> 1.47 us
  Pallas kernels: 44.2 us -> 42.1 us
  other arithmetic: 0.83 us -> 0 us
    unnamed x6 -> x1, local copies, waits for them, and re-layouts: 8.15 us -> 1.47 us
    pallas_call x1, Pallas kernels: 44.2 us -> 42.1 us  [shards(): call(jnp.swapaxes(latent, 1, 2), jnp.swapaxes(cached_latent, 2, 3), cache...]
    broadcast_in_dim x2 -> x0, local copies, waits for them, and re-layouts: 1.83 us -> none  [the longest x1 1.24 us: shards(): norm_gain[None, :]]
    pallas_call x1 -> x0, local copies, waits for them, and re-layouts: 1.6 us -> none  [shards(): call(latent, cached_latent, cached_features, reward_grad, conv_in_weight,...]
    concatenate x1 -> x0, other arithmetic: 0.83 us -> none  [shards(): jnp.concatenate([out_gain, out_gain])[None, :]]
where the time goes in v1:
time: 43.7 us; the launch traced here: 43.6 us
  Pallas kernels  42.1 us (96%)
  local copies, waits for them, and re-layouts  1.47 us (3%)
    pallas_call x1, Pallas kernels, shards(): call(jnp.swapaxes(latent, 1, 2), jnp.swapaxes(cached_latent, 2, 3), cache...  42.1 us
    unnamed x1, local copies, waits for them, and re-layouts  1.47 us

profile of v1, /device:TPU:1, one launch (start us, length us, event | category | flops | bytes accessed | tf_op | source)
XLA Modules:
  0.0 43.6 jit_solution(497213463022160135)
XLA Ops:
  0.0 42.1 %shard_map.100 = f32[64,160]{1,0:T(8,128)} custom-call(bf16[4,16,160]{2,1,0:T(8,128)(2,1)} %bitcast.9, bf16[2,4,16,160]{3,2,1,0:T(8,128)(2,1)} %bitcast.8, bf16[2,4,160,384]{3,2,1,0:T(8,128)(2,1)} %feat_in.1, bf16[8,192,320]{2,1,0:T(8,128)(2,1)} %bitcast.6, bf16[3,3,3,16,384]{4,3,2,1,0:T(8,128)(2,1)} %win_in.1, bf16[3,3,3,384,384]{4,3,2,1,0:T(8,128)(2,1)} %wmid_in.1, ...), custom_call_target="tpu_custom_call" | custom-call | tf_op jit(solution)/shard_map/pallas_call | solution.py:454
  42.1 1.5 %copy.12 = f32[160,64]{0,1:T(8,128)} copy(f32[160,64]{0,1:T(8,128)} %bitcast.7) | data formatting | bytes 81920

commit v2 on v1

v2 whole, which is shorter than its diff:
```python
import jax
import jax.numpy as jnp
from jax import lax
from jax.experimental import pallas as pl
from jax.experimental.pallas import tpu as pltpu
from jax.sharding import PartitionSpec as P

EPS = 1e-06
F32 = jnp.float32
BF16 = jnp.bfloat16
ROWS = 4
COLS = 160
LAT = 16
MID = 384
OUT = 192
TILES = 32
PIECE = 5
TOK = 80
VMEM_LIMIT = 60 << 20


def hops(k):
    z = (k // 2) % 8
    return min(z, 8 - z) + (1 if 8 <= k < 24 else 0)


FAR_FIRST = sorted(range(1, TILES), key=lambda k: -hops(k))


def iota(shape, dim):
    return lax.broadcasted_iota(jnp.int32, shape, dim)


def down(x):
    return jnp.where(iota(x.shape, 0) == 0, 0.0, pltpu.roll(x, 1, 0))


def up(x):
    n = x.shape[0]
    return jnp.where(iota(x.shape, 0) == n - 1, 0.0, pltpu.roll(x, n - 1, 0))


def mixed(x, low, high):
    a, b, c = x[:, :128], x[:, 128:256], x[:, 256:]
    middle = jnp.where(iota(b.shape, 1) < 64, low(b), high(b))
    return jnp.concatenate([low(a), middle, high(c)], axis=1)


def halves_mean(x):
    a, b, c = x[:, :128], x[:, 128:256], x[:, 256:]
    left = iota(b.shape, 1) < 64
    first = jnp.sum(a + jnp.where(left, b, 0.0), axis=1, keepdims=True) * (1.0 / OUT)
    second = jnp.sum(c + jnp.where(left, 0.0, b), axis=1, keepdims=True) * (1.0 / OUT)
    return first, second


def spread(first, second, rows):
    left = iota((rows, 128), 1) < 64
    one = jnp.broadcast_to(first, (rows, 128))
    two = jnp.broadcast_to(second, (rows, 128))
    return jnp.concatenate([one, jnp.where(left, one, two), two], axis=1)


def cotangent(normed, half_gain, grad):
    q = normed * half_gain
    t = jnp.tanh(q)
    return (grad * half_gain) * ((1.0 + t) * (1.0 + q * (1.0 - t)))


def dot(a, b):
    return jnp.dot(a, b, preferred_element_type=F32)


def dot_t(a, b):
    return lax.dot_general(a, b, (((1,), (1,)), ((), ())), preferred_element_type=F32)


def kernel(
    lat_in, latc_in, feat_in, rew_in, win_in, wmid_in, wup_in, gain_in, ogain_in, order_in,
    out_ref,
    lat, feat, hid, xs, rew, rewp, win, wmid, wback, wup, fold, vt,
    psend, precv, bg, zs, tsend, trecv, place, acc, gain_ref, ogain_ref, order_ref,
    local_sem, halo_send, halo_recv, x_send, x_recv, p_send, p_recv, b_send, b_recv,
    t_send, t_recv, know_sem,
):
    me = lax.axis_index("tile")

    def at(offset):
        return {"tile": lax.rem(me + (offset + TILES), TILES)}

    def signal(sem, offset):
        pl.semaphore_signal(sem, inc=1, device_id=at(offset), device_id_type=pl.DeviceIdType.MESH)

    def remote(src, dst, send, recv, offset):
        return pltpu.make_async_remote_copy(
            src_ref=src, dst_ref=dst, send_sem=send, recv_sem=recv,
            device_id=at(offset), device_id_type=pl.DeviceIdType.MESH,
        )

    local = []

    def load(src, dst):
        copy = pltpu.make_async_copy(src, dst, local_sem.at[len(local)])
        copy.start()
        local.append(copy)
        return copy

    barrier = pltpu.get_barrier_semaphore()
    signal(barrier, -1)
    signal(barrier, 1)
    load_lat = [
        load(lat_in, lat.at[2, pl.ds(2, ROWS)]),
        load(latc_in, lat.at[pl.ds(0, 2), pl.ds(2, ROWS)]),
    ]
    load_win = load(win_in, win)
    load_wup = load(wup_in, wup)
    load_rew = load(rew_in, rew)
    load_feat = load(feat_in, feat.at[pl.ds(0, 2), pl.ds(1, ROWS)])
    load_small = [load(gain_in, gain_ref), load(ogain_in, ogain_ref), load(order_in, order_ref)]
    load_mid = []
    for t in (0, 1, 2):
        for j in range(3):
            load_mid.append(load(wmid_in.at[t, :, j], wmid.at[t, :, :, pl.ds(j * MID, MID)]))
    load_back = []
    for i in range(3):
        load_back.append(load(wmid_in.at[2, i], wback.at[:, :, pl.ds(i * MID, MID)]))

    pl.semaphore_wait(barrier, 2)
    halo = []
    for side, offset in ((0, -1), (1, 1)):
        row = 0 if side == 0 else ROWS - 2
        land = ROWS + 2 if side == 0 else 0
        copies = [
            remote(lat_in.at[pl.ds(row, 2)], lat.at[2, pl.ds(land, 2)],
                   halo_send.at[side, 0], halo_recv.at[side, 0], offset),
            remote(latc_in.at[:, pl.ds(row, 2)], lat.at[pl.ds(0, 2), pl.ds(land, 2)],
                   halo_send.at[side, 1], halo_recv.at[side, 1], offset),
        ]
        row = 0 if side == 0 else ROWS - 1
        land = ROWS + 1 if side == 0 else 0
        copies.append(
            remote(feat_in.at[:, pl.ds(row, 1)], feat.at[pl.ds(0, 2), pl.ds(land, 1)],
                   halo_send.at[side, 2], halo_recv.at[side, 2], offset))
        halo.append(copies)
    for n in range(3):
        for side in range(2):
            halo[side][n].start()
    signal(know_sem.at[0], -1)
    signal(know_sem.at[0], 1)

    load_wup.wait()
    parts = []
    for i in range(3):
        k0, k1, k2 = (wup[i, j].astype(F32) for j in range(3))
        parts.append(jnp.concatenate([k0, k2, k1 + k2, k0 + k1], axis=0))
    fold[0, :, :MID] = parts[0].astype(BF16)
    fold[0, :, MID:] = (parts[1] + parts[2]).astype(BF16)
    fold[1, :, :MID] = (parts[0] + parts[1]).astype(BF16)
    fold[1, :, MID:] = parts[2].astype(BF16)

    load_rew.wait()
    n = iota((2 * COLS, 2 * COLS), 0)
    column = jnp.where(n < COLS, 2 * n, 2 * n - (2 * COLS - 1))
    parting = jnp.where(iota((2 * COLS, 2 * COLS), 1) == column, 1.0, 0.0).astype(BF16)
    left = iota((COLS, 128), 1) < 64
    for y in range(2 * ROWS):
        flat = jnp.concatenate([rew[y], jnp.zeros((256 - OUT, 2 * COLS), BF16)], axis=0)
        parted = dot_t(parting, flat)
        even, odd = parted[:COLS], parted[COLS:]
        o0, o1 = pltpu.roll(odd[:, :128], 64, 1), pltpu.roll(odd[:, 128:], 64, 1)
        rewp[y] = jnp.concatenate(
            [even[:, :128], jnp.where(left, even[:, 128:], o0), jnp.where(left, o0, o1)],
            axis=1).astype(BF16)

    for copy in load_lat + load_mid[:3] + [load_win, load_feat] + load_small:
        copy.wait()
    for n in range(2):
        for side in range(2):
            halo[side][n].wait_recv()

    @pl.when(me == 0)
    def _():
        lat[:, 0:2] = jnp.zeros((3, 2, LAT, COLS), BF16)

    @pl.when(me == TILES - 1)
    def _():
        lat[:, ROWS + 2:] = jnp.zeros((3, 2, LAT, COLS), BF16)

    def frames(rows, times):
        return jnp.concatenate(
            [jnp.concatenate([feat[t, h + i] for t in times for i in range(3)], axis=1)
             for h in rows], axis=0)

    taps = []
    for h in range(ROWS + 4):
        x = jnp.concatenate([lat[t, h].astype(F32) for t in range(3)], axis=0).T
        taps.append(jnp.concatenate([down(x), x, up(x)], axis=1).astype(BF16))
    total = None
    for i in range(3):
        weight = jnp.concatenate([win[t, i, j] for j in range(3) for t in range(3)], axis=0)
        part = dot(jnp.concatenate(taps[i:i + ROWS + 2], axis=0), weight)
        total = part if total is None else total + part
    acc[...] = dot(frames((1, 2), (0,)), wmid[0].reshape(3 * MID, 3 * MID))
    half_gain = gain_ref[...].reshape(1, MID) * 0.5
    for h in range(ROWS + 2):
        value = total[h * COLS:(h + 1) * COLS].astype(BF16)
        hid[h] = value
        v = value.astype(F32)
        q = v * lax.rsqrt(jnp.mean(v * v, axis=1, keepdims=True) + EPS) * half_gain
        feat[2, h] = (q + q * jnp.tanh(q)).astype(BF16)

    for side in range(2):
        halo[side][2].wait_recv()

    @pl.when(me == 0)
    def _():
        feat[:, 0] = jnp.zeros((3, COLS, MID), BF16)

    @pl.when(me == TILES - 1)
    def _():
        feat[:, ROWS + 1] = jnp.zeros((3, COLS, MID), BF16)

    for copy in load_mid[3:]:
        copy.wait()
    pl.semaphore_wait(know_sem.at[0], 2)
    signal(know_sem.at[1], -2)
    signal(know_sem.at[1], 2)

    def middle(rows, times, start=None):
        depth = 3 * MID * len(times)
        y = dot(frames(rows, times), wmid[times[0]:].reshape(depth, 3 * MID))
        if start is not None:
            y = y + start[...]
        for n, h in enumerate(rows):
            z = y[n * COLS:(n + 1) * COLS]
            value = z[:, MID:2 * MID] + down(z[:, :MID]) + up(z[:, 2 * MID:])
            xs[h + 1] = (hid[h + 1].astype(F32) + value).astype(BF16)

    middle((0, 3), (0, 1, 2))
    x_up = remote(xs.at[1], xs.at[ROWS + 1], x_send.at[0], x_recv.at[0], -1)
    x_down = remote(xs.at[ROWS], xs.at[0], x_send.at[1], x_recv.at[1], 1)
    x_up.start()
    x_down.start()
    pl.semaphore_wait(know_sem.at[1], 2)
    signal(know_sem.at[2], -4)
    signal(know_sem.at[2], 4)
    middle((1, 2), (1, 2), acc)
    pl.semaphore_wait(know_sem.at[2], 2)
    signal(know_sem.at[3], -8)
    signal(know_sem.at[3], 8)
    x_up.wait_recv()
    x_down.wait_recv()

    @pl.when(me == 0)
    def _():
        xs[0] = jnp.zeros((COLS, MID), BF16)

    @pl.when(me == TILES - 1)
    def _():
        xs[ROWS + 1] = jnp.zeros((COLS, MID), BF16)

    half_ogain = ogain_ref[...].reshape(1, OUT) * 0.5
    half_ogain = jnp.concatenate([half_ogain, half_ogain], axis=1)

    def forward(a, rows):
        left = jnp.concatenate(
            [jnp.concatenate([xs[h + a], xs[h + a + 1]], axis=1) for h in rows], axis=0)
        return dot_t(left, fold[a])

    def pull(a, rows, y):
        lefts = []
        for n, h in enumerate(rows):
            z = y[n * COLS:(n + 1) * COLS]
            v = (z[:, MID:] + mixed(z[:, :MID], down, up)).astype(BF16).astype(F32)
            one, two = halves_mean(v * v)
            scale = spread(lax.rsqrt(one + EPS), lax.rsqrt(two + EPS), COLS)
            normed = v * scale
            t = cotangent(normed, half_ogain, rewp[2 * h + a].astype(F32))
            one, two = halves_mean(t * normed)
            g = scale * (t - normed * spread(one, two, COLS))
            lefts.append(jnp.concatenate([mixed(g, up, down), g], axis=1).astype(BF16))
        return jnp.concatenate(lefts, axis=0)

    def back(a, rows, left):
        z = dot(left, fold[a])
        return {h: (z[n * COLS:(n + 1) * COLS, :MID], z[n * COLS:(n + 1) * COLS, MID:])
                for n, h in enumerate(rows)}

    batches = ((0, (0, 1)), (1, (2, 3)), (0, (2, 3)), (1, (0, 1)))
    zz = [{}, {}]
    sent = []
    y = forward(*batches[0])
    for n, (a, rows) in enumerate(batches):
        following = forward(*batches[n + 1]) if n < 3 else None
        zz[a].update(back(a, rows, pull(a, rows, y)))
        y = following
        if n < 2:
            psend[n] = (zz[0][0][0] if n == 0 else zz[1][3][1]).astype(BF16)
            copy = remote(psend.at[n], precv.at[1 - n], p_send.at[n], p_recv.at[n], 2 * n - 1)
            copy.start()
            sent.append(copy)
    z0, z1 = zz
    p_up, p_down = sent
    p_up.wait_recv()
    p_down.wait_recv()

    @pl.when(me == 0)
    def _():
        precv[0] = jnp.zeros((COLS, MID), BF16)

    @pl.when(me == TILES - 1)
    def _():
        precv[1] = jnp.zeros((COLS, MID), BF16)

    bg[1] = (z0[0][1] + z0[1][0] + z1[0][0] + precv[0].astype(F32)).astype(BF16)
    bg[ROWS] = (z0[3][1] + precv[1].astype(F32) + z1[3][0] + z1[2][1]).astype(BF16)
    b_up = remote(bg.at[1], bg.at[ROWS + 1], b_send.at[0], b_recv.at[0], -1)
    b_down = remote(bg.at[ROWS], bg.at[0], b_send.at[1], b_recv.at[1], 1)
    b_up.start()
    b_down.start()
    for h in (1, 2):
        bg[h + 1] = (z0[h][1] + z0[h + 1][0] + z1[h][0] + z1[h - 1][1]).astype(BF16)

    r = iota((1024, 144), 0)
    par = lax.shift_right_logical(r, 9)
    d = lax.shift_right_logical(r, 7) & 3
    d = jnp.where(d == 3, -1, d)
    extra = lax.shift_right_logical(r, 6) & 1
    a = lax.shift_right_logical(r, 5) & 1
    b = lax.shift_right_logical(r, 4) & 1
    c = r & 15
    i = jnp.where(extra == 0, jnp.where(par == 0, a + 1, a), jnp.where(par == 0, 0, 2))
    fits = jnp.where(extra == 0, 1, jnp.where(par == 0, a, 1 - a))
    j = b - d + 1
    fits = jnp.where((j >= 0) & (j <= 2), fits, 0)
    want = jnp.where(fits == 1, i * 48 + j * 16 + c, -1)
    pick = jnp.where(iota((1024, 144), 1) == want, 1.0, 0.0).astype(BF16)
    vt[...] = dot(pick, win[2].reshape(144, MID)).astype(BF16)
    zs[:, :, 0:8] = jnp.zeros((ROWS, 4, 8, 128), F32)
    zs[:, :, COLS + 8:] = jnp.zeros((ROWS, 4, 8, 128), F32)

    for copy in load_back:
        copy.wait()

    def lower(rows):
        left = jnp.concatenate(
            [jnp.concatenate([bg[h + 2], bg[h + 1], bg[h]], axis=1) for h in rows], axis=0)
        y = dot_t(left, wback[...].reshape(3 * MID, 3 * MID))
        for n, h in enumerate(rows):
            z = y[n * COLS:(n + 1) * COLS]
            grad = z[:, MID:2 * MID] + up(z[:, :MID]) + down(z[:, 2 * MID:])
            v = hid[h + 1].astype(F32)
            scale = lax.rsqrt(jnp.mean(v * v, axis=1, keepdims=True) + EPS)
            normed = v * scale
            t = cotangent(normed, half_gain, grad)
            m = jnp.mean(t * normed, axis=1, keepdims=True)
            g = (bg[h + 1].astype(F32) + scale * (t - normed * m)).astype(BF16)
            last = dot_t(g, vt[(h % 2) * 512:(h % 2) * 512 + 512])
            for p in range(4):
                zs[h, p, 8:COLS + 8] = last[:, p * 128:(p + 1) * 128]

    lower((1, 2))
    b_up.wait_recv()
    b_down.wait_recv()

    @pl.when(me == 0)
    def _():
        bg[0] = jnp.zeros((COLS, MID), BF16)

    @pl.when(me == TILES - 1)
    def _():
        bg[ROWS + 1] = jnp.zeros((COLS, MID), BF16)

    lower((0, 3))

    def tokens(h):
        picks = ((0, 0), (1, 1), (2, 2), (3, -1))
        parts = [zs[h, n, pl.ds(8 + d, TOK, stride=2), :] for n, d in picks]
        return (parts[0] + parts[1]) + (parts[2] + parts[3])

    u0, u1, u2, u3 = (tokens(h) for h in range(ROWS))
    low = iota((TOK, 128), 1) < 64
    m0 = jnp.where(low, u0 + u1 + pltpu.roll(u2, 64, 1), u3)
    m1 = jnp.where(low, u2 + u3 + pltpu.roll(u1, 64, 1), u0)
    both = jnp.concatenate([m0, m1], axis=0).astype(BF16)
    row = iota((256, TILES * PIECE), 0)
    source = lax.shift_right_logical(row, 3) * PIECE + (row & 7)
    take = ((row & 7) < PIECE) & (iota((256, TILES * PIECE), 1) == source)
    blocks = dot(jnp.where(take, 1.0, 0.0).astype(BF16), both)
    tsend[...] = blocks.reshape(TILES, 8, 128).astype(BF16)

    pl.semaphore_wait(know_sem.at[3], 2)

    def block_copy(k):
        to = lax.rem(me + k, TILES)
        return pltpu.make_async_remote_copy(
            src_ref=tsend.at[to], dst_ref=trecv.at[me], send_sem=t_send.at[k],
            recv_sem=t_recv.at[k],
            device_id={"tile": to}, device_id_type=pl.DeviceIdType.MESH)

    for k in FAR_FIRST:
        block_copy(k).start()
    trecv[me] = tsend[me]

    slot = lax.shift_right_logical(iota((256, 1), 0), 3)
    own_at = jnp.full((256, 1), -1, jnp.int32)
    edge_at = jnp.full((256, 1), -1, jnp.int32)
    for t in range(TILES):
        own_at = jnp.where(slot == t, order_ref[t], own_at)
        after = order_ref[t + 1] if t + 1 < TILES else jnp.int32(-1)
        before = order_ref[t - 1] if t > 0 else jnp.int32(-1)
        edge_at = jnp.where(slot == t, jnp.where(me < TILES // 2, after, before), edge_at)
    spot = iota((256, TILES * PIECE), 1)
    block = lax.shift_right_logical(spot * 205, 10)
    same = (spot - block * PIECE) == (iota((256, TILES * PIECE), 0) & 7)
    place[0] = jnp.where(same & (block == own_at), 1.0, 0.0).astype(BF16)
    place[1] = jnp.where(same & (block == edge_at), 1.0, 0.0).astype(BF16)

    for k in range(1, TILES):
        source = lax.rem(me + (TILES - k), TILES)
        pltpu.make_async_remote_copy(
            src_ref=tsend.at[source], dst_ref=trecv.at[source], send_sem=t_send.at[k],
            recv_sem=t_recv.at[k],
            device_id={"tile": source}, device_id_type=pl.DeviceIdType.MESH).wait_recv()
    got = trecv[...].astype(F32).reshape(TILES * 8, 128).T.astype(BF16)
    out_ref[...] = dot(got[:64], place[0]) + dot(got[64:], place[1])

    for copies in halo:
        for copy in copies:
            copy.wait_send()
    for copy in (x_up, x_down, p_up, p_down, b_up, b_down):
        copy.wait_send()
    for k in range(1, TILES):
        block_copy(k).wait_send()


def shards(latent, cached_latent, cached_features, reward_grad, conv_in_weight, conv_mid_weight,
           conv_up_weight, norm_gain, out_gain, shard_order):
    hbm = pl.BlockSpec(memory_space=pltpu.HBM)
    dma = pltpu.SemaphoreType.DMA
    call = pl.pallas_call(
        kernel,
        out_shape=pltpu.VMEM((4 * LAT, TILES * PIECE), F32),
        in_specs=[hbm] * 10,
        out_specs=pl.BlockSpec(memory_space=pltpu.VMEM),
        scratch_shapes=[
            pltpu.VMEM((3, ROWS + 4, LAT, COLS), BF16),
            pltpu.VMEM((3, ROWS + 2, COLS, MID), BF16),
            pltpu.VMEM((ROWS + 2, COLS, MID), BF16),
            pltpu.VMEM((ROWS + 2, COLS, MID), BF16),
            pltpu.VMEM((2 * ROWS, OUT, 2 * COLS), BF16),
            pltpu.VMEM((2 * ROWS, COLS, 2 * OUT), BF16),
            pltpu.VMEM((3, 3, 3, LAT, MID), BF16),
            pltpu.VMEM((3, 3, MID, 3 * MID), BF16),
            pltpu.VMEM((3, MID, 3 * MID), BF16),
            pltpu.VMEM((3, 3, OUT, MID), BF16),
            pltpu.VMEM((2, 4 * OUT, 2 * MID), BF16),
            pltpu.VMEM((1024, MID), BF16),
            pltpu.VMEM((2, COLS, MID), BF16),
            pltpu.VMEM((2, COLS, MID), BF16),
            pltpu.VMEM((ROWS + 2, COLS, MID), BF16),
            pltpu.VMEM((ROWS, 4, COLS + 16, 128), F32),
            pltpu.VMEM((TILES, 8, 128), BF16),
            pltpu.VMEM((TILES, 8, 128), BF16),
            pltpu.VMEM((2, 256, TILES * PIECE), BF16),
            pltpu.VMEM((2 * COLS, 3 * MID), F32),
            pltpu.VMEM((MID,), F32), pltpu.VMEM((OUT,), F32), pltpu.SMEM((TILES,), jnp.int32),
            dma((24,)), dma((2, 3)), dma((2, 3)), dma((2,)), dma((2,)), dma((2,)), dma((2,)),
            dma((2,)), dma((2,)), dma((TILES,)), dma((TILES,)),
            pltpu.SemaphoreType.REGULAR((4,)),
        ],
        compiler_params=pltpu.CompilerParams(
            collective_id=0, has_side_effects=True, vmem_limit_bytes=VMEM_LIMIT),
    )
    out = call(jnp.swapaxes(latent, 1, 2), jnp.swapaxes(cached_latent, 2, 3), cached_features,
               jnp.swapaxes(reward_grad, 1, 2), conv_in_weight, conv_mid_weight,
               jnp.swapaxes(conv_up_weight, 2, 3), norm_gain, out_gain, shard_order)
    return out.T


def solution(mesh):
    part = P(("prompt", "tile"), None, None)
    frames = P(None, ("prompt", "tile"), None, None)
    return jax.shard_map(
        shards,
        mesh=mesh,
        in_specs=(part, frames, frames, part, P(), P(), P(), P(), P(), P("prompt")),
        out_specs=P(("prompt", "tile"), None),
        check_vma=False,
    )
```

time: 43.7 us -> 40.5 us (0.927)
  Pallas kernels: 42.1 us -> 39.8 us
  local copies, waits for them, and re-layouts: 1.47 us -> 0.63 us
    pallas_call x1, Pallas kernels: 42.1 us -> 39.8 us  [shards(): call(jnp.swapaxes(latent, 1, 2), jnp.swapaxes(cached_latent, 2, 3), cache...]
    unnamed x1, local copies, waits for them, and re-layouts: 1.47 us -> 0.63 us
where the time goes in v2:
time: 40.5 us
  Pallas kernels  39.8 us (98%)
  local copies, waits for them, and re-layouts  0.63 us (2%)
    pallas_call x1, Pallas kernels, shards(): call(jnp.swapaxes(latent, 1, 2), jnp.swapaxes(cached_latent, 2, 3), cache...  39.8 us

profile of v2, /device:TPU:1, one launch (start us, length us, event | category | flops | bytes accessed | tf_op | source)
XLA Modules:
  0.0 40.5 jit_solution(3049531730707954378)
XLA Ops:
  0.0 39.8 %shard_map.100 = f32[64,160]{1,0:T(8,128)S(1)} custom-call(bf16[4,16,160]{2,1,0:T(8,128)(2,1)} %bitcast.9, bf16[2,4,16,160]{3,2,1,0:T(8,128)(2,1)} %bitcast.8, bf16[2,4,160,384]{3,2,1,0:T(8,128)(2,1)} %feat_in.1, bf16[8,192,320]{2,1,0:T(8,128)(2,1)} %bitcast.7, bf16[3,3,3,16,384]{4,3,2,1,0:T(8,128)(2,1)} %win_in.1, bf16[3,3,3,384,384]{4,3,2,1,0:T(8,128)(2,1)} %wmid_in.1, ...), custom_call_target="tpu_custom_call" | custom-call | tf_op jit(solution)/shard_map/pallas_call | solution.py:475
  39.8 0.6 %copy.12 = f32[160,64]{0,1:T(8,128)} copy(f32[160,64]{0,1:T(8,128)S(1)} %bitcast.5) | data formatting | bytes 81920

commit v3 on v2

--- a/solution.py
+++ b/solution.py
@@ -16,6 +16,7 @@
 TILES = 32
 PIECE = 5
 TOK = 80
+CHUNKS = ((0, 256), (256, 128))
 VMEM_LIMIT = 60 << 20
 
 
@@ -79,8 +80,8 @@
     lat_in, latc_in, feat_in, rew_in, win_in, wmid_in, wup_in, gain_in, ogain_in, order_in,
     out_ref,
     lat, feat, hid, xs, rew, rewp, win, wmid, wback, wup, fold, vt,
-    psend, precv, bg, zs, tsend, trecv, place, acc, gain_ref, ogain_ref, order_ref,
-    local_sem, halo_send, halo_recv, x_send, x_recv, p_send, p_recv, b_send, b_recv,
+    bg, zs, tsend, trecv, place, acc, gain_ref, ogain_ref, order_ref,
+    local_sem, halo_send, halo_recv, x_send, x_recv, b_send, b_recv,
     t_send, t_recv, know_sem,
 ):
     me = lax.axis_index("tile")
@@ -114,17 +115,16 @@
     ]
     load_win = load(win_in, win)
     load_wup = load(wup_in, wup)
-    load_rew = load(rew_in, rew)
+    load_rew = load(rew_in, rew.at[pl.ds(1, 2 * ROWS)])
     load_feat = load(feat_in, feat.at[pl.ds(0, 2), pl.ds(1, ROWS)])
     load_small = [load(gain_in, gain_ref), load(ogain_in, ogain_ref), load(order_in, order_ref)]
     load_mid = []
     for t in (0, 1, 2):
         for j in range(3):
-            load_mid.append(load(wmid_in.at[t, :, j], wmid.at[t, :, :, pl.ds(j * MID, MID)]))
-    load_back = []
-    for i in range(3):
-        load_back.append(load(wmid_in.at[2, i], wback.at[:, :, pl.ds(i * MID, MID)]))
-
+            for start, width in CHUNKS:
+                load_mid.append(load(
+                    wmid_in.at[t, :, j, :, pl.ds(start, width)],
+                    wmid.at[t, :, :, pl.ds(3 * start + j * width, width)]))
     pl.semaphore_wait(barrier, 2)
     halo = []
     for side, offset in ((0, -1), (1, 1)):
@@ -141,8 +141,13 @@
         copies.append(
             remote(feat_in.at[:, pl.ds(row, 1)], feat.at[pl.ds(0, 2), pl.ds(land, 1)],
                    halo_send.at[side, 2], halo_recv.at[side, 2], offset))
+        row = 0 if side == 0 else 2 * ROWS - 1
+        land = 2 * ROWS + 1 if side == 0 else 0
+        copies.append(
+            remote(rew_in.at[pl.ds(row, 1)], rew.at[pl.ds(land, 1)],
+                   halo_send.at[side, 3], halo_recv.at[side, 3], offset))
         halo.append(copies)
-    for n in range(3):
+    for n in range(4):
         for side in range(2):
             halo[side][n].start()
     signal(know_sem.at[0], -1)
@@ -163,16 +168,20 @@
     column = jnp.where(n < COLS, 2 * n, 2 * n - (2 * COLS - 1))
     parting = jnp.where(iota((2 * COLS, 2 * COLS), 1) == column, 1.0, 0.0).astype(BF16)
     left = iota((COLS, 128), 1) < 64
-    for y in range(2 * ROWS):
-        flat = jnp.concatenate([rew[y], jnp.zeros((256 - OUT, 2 * COLS), BF16)], axis=0)
-        parted = dot_t(parting, flat)
-        even, odd = parted[:COLS], parted[COLS:]
-        o0, o1 = pltpu.roll(odd[:, :128], 64, 1), pltpu.roll(odd[:, 128:], 64, 1)
-        rewp[y] = jnp.concatenate(
-            [even[:, :128], jnp.where(left, even[:, 128:], o0), jnp.where(left, o0, o1)],
-            axis=1).astype(BF16)
-
-    for copy in load_lat + load_mid[:3] + [load_win, load_feat] + load_small:
+
+    def part_columns(ys):
+        for y in ys:
+            flat = jnp.concatenate([rew[y], jnp.zeros((256 - OUT, 2 * COLS), BF16)], axis=0)
+            parted = dot_t(parting, flat)
+            even, odd = parted[:COLS], parted[COLS:]
+            o0, o1 = pltpu.roll(odd[:, :128], 64, 1), pltpu.roll(odd[:, 128:], 64, 1)
+            rewp[y] = jnp.concatenate(
+                [even[:, :128], jnp.where(left, even[:, 128:], o0), jnp.where(left, o0, o1)],
+                axis=1).astype(BF16)
+
+    part_columns(range(1, 2 * ROWS + 1))
+
+    for copy in load_lat + load_mid[:6] + [load_win, load_feat] + load_small:
         copy.wait()
     for n in range(2):
         for side in range(2):
@@ -220,45 +229,43 @@
     def _():
         feat[:, ROWS + 1] = jnp.zeros((3, COLS, MID), BF16)
 
-    for copy in load_mid[3:]:
+    for copy in load_mid[6:]:
         copy.wait()
+    load_back = []
+    for i in range(3):
+        load_back.append(load(wmid_in.at[2, i], wback.at[:, :, pl.ds(i * MID, MID)]))
     pl.semaphore_wait(know_sem.at[0], 2)
     signal(know_sem.at[1], -2)
     signal(know_sem.at[1], 2)
 
-    def middle(rows, times, start=None):
+    def middle(rows, times, chunk, first=None):
+        start, width = chunk
         depth = 3 * MID * len(times)
-        y = dot(frames(rows, times), wmid[times[0]:].reshape(depth, 3 * MID))
-        if start is not None:
-            y = y + start[...]
+        lanes = slice(3 * start, 3 * (start + width))
+        y = dot(frames(rows, times), wmid[times[0]:, :, :, lanes].reshape(depth, 3 * width))
+        if first is not None:
+            y = y + first[:, lanes]
         for n, h in enumerate(rows):
             z = y[n * COLS:(n + 1) * COLS]
-            value = z[:, MID:2 * MID] + down(z[:, :MID]) + up(z[:, 2 * MID:])
-            xs[h + 1] = (hid[h + 1].astype(F32) + value).astype(BF16)
-
-    middle((0, 3), (0, 1, 2))
-    x_up = remote(xs.at[1], xs.at[ROWS + 1], x_send.at[0], x_recv.at[0], -1)
-    x_down = remote(xs.at[ROWS], xs.at[0], x_send.at[1], x_recv.at[1], 1)
-    x_up.start()
-    x_down.start()
+            value = z[:, width:2 * width] + down(z[:, :width]) + up(z[:, 2 * width:])
+            held = hid[h + 1, :, start:start + width].astype(F32)
+            xs[h + 1, :, start:start + width] = (held + value).astype(BF16)
+
+    x_copies = []
+    for n, (start, width) in enumerate(CHUNKS):
+        middle((0, 3), (0, 1, 2), (start, width))
+        part = pl.ds(start, width)
+        x_copies.append(remote(xs.at[1, :, part], xs.at[ROWS + 1, :, part],
+                               x_send.at[n, 0], x_recv.at[n, 0], -1))
+        x_copies.append(remote(xs.at[ROWS, :, part], xs.at[0, :, part],
+                               x_send.at[n, 1], x_recv.at[n, 1], 1))
+        x_copies[-2].start()
+        x_copies[-1].start()
+    for chunk in CHUNKS:
+        middle((1, 2), (1, 2), chunk, acc)
     pl.semaphore_wait(know_sem.at[1], 2)
     signal(know_sem.at[2], -4)
     signal(know_sem.at[2], 4)
-    middle((1, 2), (1, 2), acc)
-    pl.semaphore_wait(know_sem.at[2], 2)
-    signal(know_sem.at[3], -8)
-    signal(know_sem.at[3], 8)
-    x_up.wait_recv()
-    x_down.wait_recv()
-
-    @pl.when(me == 0)
-    def _():
-        xs[0] = jnp.zeros((COLS, MID), BF16)
-
-    @pl.when(me == TILES - 1)
-    def _():
-        xs[ROWS + 1] = jnp.zeros((COLS, MID), BF16)
-
     half_ogain = ogain_ref[...].reshape(1, OUT) * 0.5
     half_ogain = jnp.concatenate([half_ogain, half_ogain], axis=1)
 
@@ -275,49 +282,66 @@
             one, two = halves_mean(v * v)
             scale = spread(lax.rsqrt(one + EPS), lax.rsqrt(two + EPS), COLS)
             normed = v * scale
-            t = cotangent(normed, half_ogain, rewp[2 * h + a].astype(F32))
+            t = cotangent(normed, half_ogain, rewp[2 * h + a + 1].astype(F32))
             one, two = halves_mean(t * normed)
             g = scale * (t - normed * spread(one, two, COLS))
             lefts.append(jnp.concatenate([mixed(g, up, down), g], axis=1).astype(BF16))
         return jnp.concatenate(lefts, axis=0)
 
+    z0, z1 = zz = [{}, {}]
+
     def back(a, rows, left):
         z = dot(left, fold[a])
-        return {h: (z[n * COLS:(n + 1) * COLS, :MID], z[n * COLS:(n + 1) * COLS, MID:])
-                for n, h in enumerate(rows)}
-
-    batches = ((0, (0, 1)), (1, (2, 3)), (0, (2, 3)), (1, (0, 1)))
-    zz = [{}, {}]
-    sent = []
-    y = forward(*batches[0])
-    for n, (a, rows) in enumerate(batches):
-        following = forward(*batches[n + 1]) if n < 3 else None
-        zz[a].update(back(a, rows, pull(a, rows, y)))
-        y = following
-        if n < 2:
-            psend[n] = (zz[0][0][0] if n == 0 else zz[1][3][1]).astype(BF16)
-            copy = remote(psend.at[n], precv.at[1 - n], p_send.at[n], p_recv.at[n], 2 * n - 1)
-            copy.start()
-            sent.append(copy)
-    z0, z1 = zz
-    p_up, p_down = sent
-    p_up.wait_recv()
-    p_down.wait_recv()
+        for n, h in enumerate(rows):
+            z_row = z[n * COLS:(n + 1) * COLS]
+            zz[a][h] = (z_row[:, :MID], z_row[:, MID:])
+
+    y0 = forward(0, (1, 3))
+    y1 = forward(1, (0, 2))
+    back(0, (1, 3), pull(0, (1, 3), y0))
+    back(1, (0, 2), pull(1, (0, 2), y1))
+    for side in range(2):
+        halo[side][3].wait_recv()
 
     @pl.when(me == 0)
     def _():
-        precv[0] = jnp.zeros((COLS, MID), BF16)
+        rew[0] = jnp.zeros((OUT, 2 * COLS), BF16)
 
     @pl.when(me == TILES - 1)
     def _():
-        precv[1] = jnp.zeros((COLS, MID), BF16)
-
-    bg[1] = (z0[0][1] + z0[1][0] + z1[0][0] + precv[0].astype(F32)).astype(BF16)
-    bg[ROWS] = (z0[3][1] + precv[1].astype(F32) + z1[3][0] + z1[2][1]).astype(BF16)
+        rew[2 * ROWS + 1] = jnp.zeros((OUT, 2 * COLS), BF16)
+
+    part_columns((0, 2 * ROWS + 1))
+    for copy in x_copies:
+        copy.wait_recv()
+
+    @pl.when(me == 0)
+    def _():
+        xs[0] = jnp.zeros((COLS, MID), BF16)
+
+    @pl.when(me == TILES - 1)
+    def _():
+        xs[ROWS + 1] = jnp.zeros((COLS, MID), BF16)
+
+    y1 = forward(1, (-1, 3))
+    y0 = forward(0, (0, 4))
+    left1 = pull(1, (-1, 3), y1)
+    first = z0[1][0] + z1[0][0] + dot(left1[:COLS], fold[1, :, MID:])
+    last = z0[3][1] + z1[2][1] + dot(left1[COLS:], fold[1, :, :MID])
+    left0 = pull(0, (0, 4), y0)
+    bg[1] = (first + dot(left0[:COLS], fold[0, :, MID:])).astype(BF16)
+    bg[ROWS] = (last + dot(left0[COLS:], fold[0, :, :MID])).astype(BF16)
     b_up = remote(bg.at[1], bg.at[ROWS + 1], b_send.at[0], b_recv.at[0], -1)
     b_down = remote(bg.at[ROWS], bg.at[0], b_send.at[1], b_recv.at[1], 1)
     b_up.start()
     b_down.start()
+    pl.semaphore_wait(know_sem.at[2], 2)
+    signal(know_sem.at[3], -8)
+    signal(know_sem.at[3], 8)
+    y0 = forward(0, (2,))
+    y1 = forward(1, (1,))
+    back(0, (2,), pull(0, (2,), y0))
+    back(1, (1,), pull(1, (1,), y1))
     for h in (1, 2):
         bg[h + 1] = (z0[h][1] + z0[h + 1][0] + z1[h][0] + z1[h - 1][1]).astype(BF16)
 
@@ -416,6 +440,14 @@
     place[0] = jnp.where(same & (block == own_at), 1.0, 0.0).astype(BF16)
     place[1] = jnp.where(same & (block == edge_at), 1.0, 0.0).astype(BF16)
 
+    for copies in halo:
+        for copy in copies:
+            copy.wait_send()
+    for copy in (*x_copies, b_up, b_down):
+        copy.wait_send()
+    for k in range(1, TILES):
+        block_copy(k).wait_send()
+
     for k in range(1, TILES):
         source = lax.rem(me + (TILES - k), TILES)
         pltpu.make_async_remote_copy(
@@ -424,14 +456,6 @@
             device_id={"tile": source}, device_id_type=pl.DeviceIdType.MESH).wait_recv()
     got = trecv[...].astype(F32).reshape(TILES * 8, 128).T.astype(BF16)
     out_ref[...] = dot(got[:64], place[0]) + dot(got[64:], place[1])
-
-    for copies in halo:
-        for copy in copies:
-            copy.wait_send()
-    for copy in (x_up, x_down, p_up, p_down, b_up, b_down):
-        copy.wait_send()
-    for k in range(1, TILES):
-        block_copy(k).wait_send()
 
 
 def shards(latent, cached_latent, cached_features, reward_grad, conv_in_weight, conv_mid_weight,
@@ -448,16 +472,14 @@
             pltpu.VMEM((3, ROWS + 2, COLS, MID), BF16),
             pltpu.VMEM((ROWS + 2, COLS, MID), BF16),
             pltpu.VMEM((ROWS + 2, COLS, MID), BF16),
-            pltpu.VMEM((2 * ROWS, OUT, 2 * COLS), BF16),
-            pltpu.VMEM((2 * ROWS, COLS, 2 * OUT), BF16),
+            pltpu.VMEM((2 * ROWS + 2, OUT, 2 * COLS), BF16),
+            pltpu.VMEM((2 * ROWS + 2, COLS, 2 * OUT), BF16),
             pltpu.VMEM((3, 3, 3, LAT, MID), BF16),
             pltpu.VMEM((3, 3, MID, 3 * MID), BF16),
             pltpu.VMEM((3, MID, 3 * MID), BF16),
             pltpu.VMEM((3, 3, OUT, MID), BF16),
             pltpu.VMEM((2, 4 * OUT, 2 * MID), BF16),
             pltpu.VMEM((1024, MID), BF16),
-            pltpu.VMEM((2, COLS, MID), BF16),
-            pltpu.VMEM((2, COLS, MID), BF16),
             pltpu.VMEM((ROWS + 2, COLS, MID), BF16),
             pltpu.VMEM((ROWS, 4, COLS + 16, 128), F32),
             pltpu.VMEM((TILES, 8, 128), BF16),
@@ -465,7 +487,7 @@
             pltpu.VMEM((2, 256, TILES * PIECE), BF16),
             pltpu.VMEM((2 * COLS, 3 * MID), F32),
             pltpu.VMEM((MID,), F32), pltpu.VMEM((OUT,), F32), pltpu.SMEM((TILES,), jnp.int32),
-            dma((24,)), dma((2, 3)), dma((2, 3)), dma((2,)), dma((2,)), dma((2,)), dma((2,)),
+            dma((40,)), dma((2, 4)), dma((2, 4)), dma((2, 2)), dma((2, 2)),
             dma((2,)), dma((2,)), dma((TILES,)), dma((TILES,)),
             pltpu.SemaphoreType.REGULAR((4,)),
         ],

time: 40.5 us -> 38.5 us (0.951)
  Pallas kernels: 39.8 us -> 37.8 us
    pallas_call x1, Pallas kernels: 39.8 us -> 37.8 us  [shards(): call(jnp.swapaxes(latent, 1, 2), jnp.swapaxes(cached_latent, 2, 3), cache...]
where the time goes in v3:
time: 38.5 us; the launch traced here: 38.4 us
  Pallas kernels  37.8 us (98%)
  local copies, waits for them, and re-layouts  0.63 us (2%)
    pallas_call x1, Pallas kernels, shards(): call(jnp.swapaxes(latent, 1, 2), jnp.swapaxes(cached_latent, 2, 3), cache...  37.8 us

profile of v3, /device:TPU:1, one launch (start us, length us, event | category | flops | bytes accessed | tf_op | source)
XLA Modules:
  0.0 38.4 jit_solution(9094216701047536105)
XLA Ops:
  0.0 37.8 %shard_map.100 = f32[64,160]{1,0:T(8,128)S(1)} custom-call(bf16[4,16,160]{2,1,0:T(8,128)(2,1)} %bitcast.9, bf16[2,4,16,160]{3,2,1,0:T(8,128)(2,1)} %bitcast.8, bf16[2,4,160,384]{3,2,1,0:T(8,128)(2,1)} %feat_in.1, bf16[8,192,320]{2,1,0:T(8,128)(2,1)} %bitcast.7, bf16[3,3,3,16,384]{4,3,2,1,0:T(8,128)(2,1)} %win_in.1, bf16[3,3,3,384,384]{4,3,2,1,0:T(8,128)(2,1)} %wmid_in.1, ...), custom_call_target="tpu_custom_call" | custom-call | tf_op jit(solution)/shard_map/pallas_call | solution.py:497
  37.8 0.6 %copy.12 = f32[160,64]{0,1:T(8,128)} copy(f32[160,64]{0,1:T(8,128)S(1)} %bitcast.5) | data formatting | bytes 81920

commit v4 on v3

--- a/solution.py
+++ b/solution.py
@@ -181,7 +181,16 @@
 
     part_columns(range(1, 2 * ROWS + 1))
 
-    for copy in load_lat + load_mid[:6] + [load_win, load_feat] + load_small:
+    def frames(rows, times):
+        return jnp.concatenate(
+            [jnp.concatenate([feat[t, h + i] for t in times for i in range(3)], axis=1)
+             for h in rows], axis=0)
+
+    for copy in load_mid[:12] + [load_feat]:
+        copy.wait()
+    acc[...] = dot(frames((1, 2), (0, 1)), wmid[0:2].reshape(6 * MID, 3 * MID))
+
+    for copy in load_lat + [load_win] + load_small:
         copy.wait()
     for n in range(2):
         for side in range(2):
@@ -194,11 +203,6 @@
     @pl.when(me == TILES - 1)
     def _():
         lat[:, ROWS + 2:] = jnp.zeros((3, 2, LAT, COLS), BF16)
-
-    def frames(rows, times):
-        return jnp.concatenate(
-            [jnp.concatenate([feat[t, h + i] for t in times for i in range(3)], axis=1)
-             for h in rows], axis=0)
 
     taps = []
     for h in range(ROWS + 4):
@@ -209,7 +213,6 @@
         weight = jnp.concatenate([win[t, i, j] for j in range(3) for t in range(3)], axis=0)
         part = dot(jnp.concatenate(taps[i:i + ROWS + 2], axis=0), weight)
         total = part if total is None else total + part
-    acc[...] = dot(frames((1, 2), (0,)), wmid[0].reshape(3 * MID, 3 * MID))
     half_gain = gain_ref[...].reshape(1, MID) * 0.5
     for h in range(ROWS + 2):
         value = total[h * COLS:(h + 1) * COLS].astype(BF16)
@@ -229,7 +232,7 @@
     def _():
         feat[:, ROWS + 1] = jnp.zeros((3, COLS, MID), BF16)
 
-    for copy in load_mid[6:]:
+    for copy in load_mid[12:]:
         copy.wait()
     load_back = []
     for i in range(3):
@@ -262,7 +265,7 @@
         x_copies[-2].start()
         x_copies[-1].start()
     for chunk in CHUNKS:
-        middle((1, 2), (1, 2), chunk, acc)
+        middle((1, 2), (2,), chunk, acc)
     pl.semaphore_wait(know_sem.at[1], 2)
     signal(know_sem.at[2], -4)
     signal(know_sem.at[2], 4)

time: 38.5 us -> 38.2 us (level)
  no operation moved by 1% of the time
where the time goes in v4:
time: 38.2 us; the launch traced here: 38.1 us
  Pallas kernels  37.5 us (98%)
  local copies, waits for them, and re-layouts  0.63 us (2%)
    pallas_call x1, Pallas kernels, shards(): call(jnp.swapaxes(latent, 1, 2), jnp.swapaxes(cached_latent, 2, 3), cache...  37.5 us

profile of v4, /device:TPU:1, one launch (start us, length us, event | category | flops | bytes accessed | tf_op | source)
XLA Modules:
  0.0 38.1 jit_solution(16799944147396162331)
XLA Ops:
  0.0 37.5 %shard_map.100 = f32[64,160]{1,0:T(8,128)S(1)} custom-call(bf16[4,16,160]{2,1,0:T(8,128)(2,1)} %bitcast.9, bf16[2,4,16,160]{3,2,1,0:T(8,128)(2,1)} %bitcast.8, bf16[2,4,160,384]{3,2,1,0:T(8,128)(2,1)} %feat_in.1, bf16[8,192,320]{2,1,0:T(8,128)(2,1)} %bitcast.7, bf16[3,3,3,16,384]{4,3,2,1,0:T(8,128)(2,1)} %win_in.1, bf16[3,3,3,384,384]{4,3,2,1,0:T(8,128)(2,1)} %wmid_in.1, ...), custom_call_target="tpu_custom_call" | custom-call | tf_op jit(solution)/shard_map/pallas_call | solution.py:500
  37.5 0.6 %copy.12 = f32[160,64]{0,1:T(8,128)} copy(f32[160,64]{0,1:T(8,128)S(1)} %bitcast.5) | data formatting | bytes 81920
